TPU v7x, 512 devices: a whole 4x8x8 slice. The times are simulated.
512 devices in a mesh: dp: 8 (over x, core), section: 4 (over z_lo), seq: 16 (over z_hi, y).
Axes of the slice: x: 4, y: 8, z: 8 (z_hi: 2, z_lo: 4; z = z_hi * 4 + z_lo), core: 2. Of those that a mesh axis runs over, the one named last changes fastest.
Arguments:
- section_inputs: bfloat16 [4, 3, 8, 2048, 768], P('section', None, 'dp', 'seq'), may hold values from -6 to 6
- cotangent: bfloat16 [3, 8, 2048, 768], P(None, 'dp', 'seq'), may hold values from -6 to 6
- conv_weight: bfloat16 [4, 3, 768, 384], P('section'), may hold values from -0.125 to 0.125
- out_weight: bfloat16 [4, 384, 768], P('section'), may hold values from -0.3125 to 0.3125
- norm_scale: float32 [4, 768], P('section'), may hold values from 0.25 to 1.75
- norm_shift: float32 [4, 768], P('section'), may hold values from -3 to 3
- inner_scale: float32 [4, 384], P('section'), may hold values from 0.25 to 1.75
- inner_shift: float32 [4, 384], P('section'), may hold values from -3 to 3
Outputs:
- grad_in: bfloat16 [4, 3, 8, 2048, 768], P('section', None, 'dp', 'seq')
- grad_conv: float32 [4, 3, 768, 384], P('section', None, 'seq')
- grad_out: float32 [4, 384, 768], P('section', None, 'seq')
All inputs are finite; a program needn't handle non-finite values.
Results may differ from a plain program's by a relative error of at most 0.025.
Values may be sent and summed in bfloat16 or wider, within the bound.
A program may use at most 64 MiB of HBM per device.

v0:
```python
import jax
import jax.numpy as jnp
from jax import lax
from jax.sharding import PartitionSpec as P

BASE_DILATION = 32


gelu_coeff = 0.7978845608028654
cubic_coeff = 0.044715


def with_halo(block, sides, width):
    for axis, dim in sides:
        count = lax.axis_size(axis)
        forward = [(i, i + 1) for i in range(count - 1)]
        backward = [(target, source) for source, target in forward]
        low = lax.ppermute(
            lax.slice_in_dim(block, block.shape[dim] - width, None, axis=dim), axis, forward
        )
        high = lax.ppermute(lax.slice_in_dim(block, 0, width, axis=dim), axis, backward)
        block = jnp.concatenate([low, block, high], axis=dim)
    return block


def shifted(value, axis, by):
    length = lax.axis_size(axis)
    pairs = [(i, i + by) for i in range(length) if 0 <= i + by < length]
    return lax.ppermute(value, axis, pairs)


def gelu_pair(inputs):
    inner_arg = gelu_coeff * (inputs + cubic_coeff * inputs * inputs * inputs)
    tanh_val = jnp.tanh(inner_arg)
    result = 0.5 * inputs * (1.0 + tanh_val)
    slope_val = 0.5 * (1.0 + tanh_val) + 0.5 * inputs * (1.0 - tanh_val * tanh_val) * gelu_coeff * (
        1.0 + 3.0 * cubic_coeff * inputs * inputs
    )
    return (result, slope_val)


def put_row(buffer, update, index, is_valid):
    current = lax.dynamic_index_in_dim(buffer, index, 0, keepdims=False)
    return lax.dynamic_update_index_in_dim(buffer, jnp.where(is_valid, update, current), index, 0)


def on_device(
    section_inputs,
    cotangent,
    conv_weight,
    out_weight,
    norm_scale,
    norm_shift,
    inner_scale,
    inner_shift,
):
    sections = lax.axis_size("section")
    windows = lax.axis_size("dp")
    section_number = lax.axis_index("section")
    inputs = section_inputs[0, :, 0]
    top_grads = cotangent[:, 0]
    micro_count, row_count, channels = inputs.shape
    convolution_kernel = conv_weight[0]
    inner_width = convolution_kernel.shape[2]
    conv_flat = convolution_kernel.reshape(3 * channels, inner_width)
    out_w = out_weight[0]
    scale_one = norm_scale[0]
    shift_one = norm_shift[0]
    scale_two = inner_scale[0]
    shift_two = inner_shift[0]
    border_margin = 2 * BASE_DILATION
    dilation_rate = BASE_DILATION * (1 + section_number % 2)
    is_last = section_number == sections - 1
    tick_count = micro_count + sections - 1
    stashed = ()

    def tick(state_in, tick_num):
        received, grads_out, acc_conv, acc_out, kept = state_in
        micro_idx = tick_num - (sections - 1 - section_number)
        is_valid = jnp.logical_and(micro_idx >= 0, micro_idx < micro_count)
        safe_idx = jnp.clip(micro_idx, 0, micro_count - 1)
        block_in = lax.dynamic_index_in_dim(inputs, safe_idx, 0, keepdims=False)
        top_grad = lax.dynamic_index_in_dim(top_grads, safe_idx, 0, keepdims=False)
        grad_top = jnp.where(is_last, top_grad, received)
        pre_norm = block_in.astype(jnp.float32) * scale_one + shift_one
        act_val, act_slope = gelu_pair(pre_norm)
        hidden = act_val.astype(jnp.bfloat16)
        padded = with_halo(hidden, (("seq", 0),), border_margin)
        tap_rows = jnp.concatenate(
            [
                lax.dynamic_slice_in_dim(
                    padded, border_margin + (tap_number - 1) * dilation_rate, row_count, 0
                )
                for tap_number in range(3)
            ],
            axis=1,
        )
        inner_pre = (
            jnp.dot(tap_rows, conv_flat, preferred_element_type=jnp.float32) * scale_two + shift_two
        )
        inner_val, inner_slope = gelu_pair(inner_pre)
        inner_act = inner_val.astype(jnp.bfloat16)
        grad_inner = lax.dot_general(
            grad_top, out_w, (((1,), (1,)), ((), ())), preferred_element_type=jnp.float32
        )
        grad_conv = (grad_inner * inner_slope * scale_two).astype(jnp.bfloat16)
        grad_pad = with_halo(grad_conv, (("seq", 0),), border_margin)
        back_taps = jnp.stack(
            [
                lax.dynamic_slice_in_dim(
                    grad_pad, border_margin - (tap_number - 1) * dilation_rate, row_count, 0
                )
                for tap_number in range(3)
            ],
            axis=1,
        )
        grad_hidden = lax.dot_general(
            back_taps,
            convolution_kernel,
            (((1, 2), (0, 2)), ((), ())),
            preferred_element_type=jnp.float32,
        )
        grad_block = (grad_top.astype(jnp.float32) + grad_hidden * act_slope * scale_one).astype(
            jnp.bfloat16
        )
        handed_forward = shifted(grad_block, "section", -1)
        grads_out = put_row(grads_out, grad_block, safe_idx, is_valid)
        masked_conv = jnp.where(is_valid, grad_conv, jnp.zeros_like(grad_conv))
        masked_top = jnp.where(is_valid, grad_top, jnp.zeros_like(grad_top))
        acc_conv = acc_conv + lax.dot_general(
            tap_rows, masked_conv, (((0,), (0,)), ((), ())), preferred_element_type=jnp.float32
        )
        acc_out = acc_out + lax.dot_general(
            inner_act, masked_top, (((0,), (0,)), ((), ())), preferred_element_type=jnp.float32
        )
        return ((handed_forward, grads_out, acc_conv, acc_out, kept), None)

    starting_value = (
        jnp.zeros((row_count, channels), jnp.bfloat16),
        jnp.zeros((micro_count, row_count, channels), jnp.bfloat16),
        jnp.zeros((3 * channels, inner_width), jnp.float32),
        jnp.zeros((inner_width, channels), jnp.float32),
        stashed,
    )
    final_state, unused = lax.scan(tick, starting_value, jnp.arange(tick_count, dtype=jnp.int32))
    received, grads_out, acc_conv, acc_out, kept = final_state
    conv_part = acc_conv.reshape(3, channels, inner_width)
    shares = (
        lax.psum_scatter(
            conv_part.astype(jnp.bfloat16), "seq", scatter_dimension=1, tiled=True
        ).astype(jnp.float32),
        lax.psum_scatter(
            acc_out.astype(jnp.bfloat16), "seq", scatter_dimension=1, tiled=True
        ).astype(jnp.float32),
    )
    conv_total, out_total = (
        lax.psum(shares[0].astype(jnp.bfloat16), "dp").astype(jnp.float32),
        lax.psum(shares[1].astype(jnp.bfloat16), "dp").astype(jnp.float32),
    )
    factor = 1.0 / float(micro_count * windows)
    return (
        grads_out.reshape(section_inputs.shape),
        (conv_total * factor)[None],
        (out_total * factor)[None],
    )


def solution(mesh):
    return jax.shard_map(
        on_device,
        mesh=mesh,
        in_specs=(
            P("section", None, "dp", "seq", None),
            P(None, "dp", "seq", None),
            P("section", None, None, None),
            P("section", None, None),
            P("section", None),
            P("section", None),
            P("section", None),
            P("section", None),
        ),
        out_specs=(
            P("section", None, "dp", "seq", None),
            P("section", None, "seq", None),
            P("section", None, "seq"),
        ),
        check_vma=False,
    )
```

profile of v0, /device:TPU:1, one launch (start us, length us, event | category | flops | bytes accessed | tf_op | source)
XLA Modules:
  0.0 784.8 jit_solution(2475013103671685619)
XLA Ops:
  8.8 229.1 %while.20 = (s32[]{:T(128)}, bf16[128,768]{1,0:T(8,128)(2,1)}, bf16[3,128,768]{2,1,0:T(8,128)(2,1)}, f32[2304,384]{1,0:T(8,128)S(1)}, f32[384,768]{1,0:T(8,128)}...) while((s32[]{:T(128)}, bf16[128,768]{1,0:T(8,128)(2,1)}, ...), condition=%wide.region_1.2_spmd.clone, body=%wide.region_0.1_spmd.clone.sunk | while | flops 843939840 | bytes 44764652 | solution.py:145
  13.8 1.3 collective-permute-start
  15.1 5.3 collective-permute-start.1
  26.6 1.3 collective-permute-start.2
  27.9 4.0 collective-permute-start.3
  31.9 1.7 convolution_add_fusion.4
  33.6 2.5 bitcast_dynamic-update-slice_fusion.2
  36.1 1.3 collective-permute-start.4
  38.1 5.3 collective-permute-done.4
  49.0 1.3 collective-permute-start
  50.3 4.6 collective-permute-start.1
  61.1 1.3 collective-permute-start.2
  62.4 4.0 collective-permute-start.3
  66.4 1.7 convolution_add_fusion.4
  68.2 2.5 bitcast_dynamic-update-slice_fusion.2
  70.7 1.3 collective-permute-start.4
  72.6 5.4 collective-permute-done.4
  85.0 5.4 collective-permute-start.1
  96.5 1.3 collective-permute-start.2
  97.8 4.6 collective-permute-start.3
  102.4 1.7 convolution_add_fusion.4
  104.2 2.5 bitcast_dynamic-update-slice_fusion.2
  108.6 4.5 collective-permute-done.4
  120.1 5.8 collective-permute-start.1
  132.1 1.3 collective-permute-start.2
  133.4 4.6 collective-permute-start.3
  138.0 1.7 convolution_add_fusion.4
  139.8 2.5 bitcast_dynamic-update-slice_fusion.2
  144.2 5.5 collective-permute-done.4
  156.7 7.4 collective-permute-start.1
  170.3 1.3 collective-permute-start.2
  171.6 9.4 %collective-permute-start.3 = (bf16[64,384]{1,0:T(8,128)(2,1)S(1)}, bf16[64,384]{1,0:T(8,128)(2,1)S(1)}, u32[]{:S(2)}, u32[]{:S(2)}) collective-permute-start(bf16[64,384]{1,0:T(8,128)(2,1)S(1)} %get-tuple-element.583), channel_id=1, source_target_pairs={{0,1},{1,2},{2,3},{3,4},{4,5},{5,6},{6,7},{7,8},{8,9},{9,10},{10,1... | collective-permute-start | bytes 147464 | tf_op jit(solution)/shard_map/while/body/eval_jaxpr/ppermute | solution.py:18
  181.0 1.7 convolution_add_fusion.4
  182.8 2.5 bitcast_dynamic-update-slice_fusion.2
  187.2 4.5 collective-permute-done.4
  198.7 10.6 %collective-permute-start.1 = (bf16[64,768]{1,0:T(8,128)(2,1)}, bf16[64,768]{1,0:T(8,128)(2,1)}, u32[]{:S(2)}, u32[]{:S(2)}) collective-permute-start(bf16[64,768]{1,0:T(8,128)(2,1)} %get-tuple-element.579), channel_id=1, source_target_pairs={{0,1},{1,2},{2,3},{3,4},{4,5},{5,6},{6,7},{7,8},{8,9},{9,10},{10,1... | collective-permute-start | bytes 294920 | tf_op jit(solution)/shard_map/while/body/eval_jaxpr/ppermute | solution.py:18
  215.4 1.3 collective-permute-start.2
  216.7 9.7 %collective-permute-start.3 = (bf16[64,384]{1,0:T(8,128)(2,1)S(1)}, bf16[64,384]{1,0:T(8,128)(2,1)S(1)}, u32[]{:S(2)}, u32[]{:S(2)}) collective-permute-start(bf16[64,384]{1,0:T(8,128)(2,1)S(1)} %get-tuple-element.583), channel_id=1, source_target_pairs={{0,1},{1,2},{2,3},{3,4},{4,5},{5,6},{6,7},{7,8},{8,9},{9,10},{10,1... | collective-permute-start | bytes 147464 | tf_op jit(solution)/shard_map/while/body/eval_jaxpr/ppermute | solution.py:18
  226.4 1.7 convolution_add_fusion.4
  228.2 2.5 bitcast_dynamic-update-slice_fusion.2
  232.6 4.6 collective-permute-done.4
  237.9 2.3 copy.11
  240.3 1.4 convert_element_type.58
  241.9 253.2 %reduce-scatter.5.cloned.1.call-done = bf16[384,48]{0,1:T(8,128)(2,1)} async-done(((bf16[384,768]{0,1:T(8,128)(2,1)}), bf16[384,48]{0,1:T(8,128)(2,1)}) %reduce-scatter.5.cloned.1.call-update) | async-done | bytes 36880 | tf_op jit(solution)/shard_map/reduce_scatter | solution.py:152
  495.1 27.9 %psum.15 = bf16[384,48]{0,1:T(8,128)(2,1)S(1)} all-reduce(bf16[384,48]{0,1:T(8,128)(2,1)} %reduce-scatter.5.cloned.1.call-done), channel_id=1, replica_groups=mesh['dp'=8,'section'=4,'seq'=16] {'dp'}, use_global_device_ids=true, to_apply=%region_5.6 | all-reduce | flops 18432 | bytes 73728 | tf_op jit(solution)/shard_map/psum | solution.py:158
  522.9 182.6 %reduce-scatter.3.cloned.1.call-done = bf16[3,48,384]{2,1,0:T(8,128)(2,1)} async-done(((bf16[3,768,384]{2,1,0:T(8,128)(2,1)}), bf16[3,48,384]{2,1,0:T(8,128)(2,1)}) %reduce-scatter.3.cloned.1.call-update) | async-done | bytes 110608 | tf_op jit(solution)/shard_map/reduce_scatter | solution.py:149
  706.2 70.4 %all-reduce.2.cloned.1.call-done = bf16[3,48,384]{2,1,0:T(8,128)(2,1)} async-done(((bf16[3,48,384]{2,1,0:T(8,128)(2,1)}), bf16[3,48,384]{2,1,0:T(8,128)(2,1)}) %all-reduce.2.cloned.1.call-update) | async-done | bytes 110608 | tf_op jit(solution)/shard_map/psum | solution.py:157
  776.6 1.6 multiply_bitcast_fusion
  (254 shorter events, 83.6 us)
Async XLA Ops:
  7.2 487.9 %reduce-scatter.5.cloned.1.call-start = ((), (), s32[]{:S(2)}) async-start(), calls=%async_computation.4 | async-start | bytes 626688 | tf_op jit(solution)/shard_map/reduce_scatter | solution.py:152
  8.8 11.6 %copy-start.7 = (s32[6]{0:T(128)}, s32[6]{0:T(128)S(1)}, u32[]{:S(2)}) copy-start(s32[6]{0:T(128)S(1)} %get-tuple-element.646) | copy-start | bytes 76 | tf_op jit(solution)/shard_map/while
  13.8 10.2 %collective-permute-start = (bf16[64,768]{1,0:T(8,128)(2,1)}, bf16[64,768]{1,0:T(8,128)(2,1)}, u32[]{:S(2)}, u32[]{:S(2)}) collective-permute-start(bf16[64,768]{1,0:T(8,128)(2,1)} %get-tuple-element.578), channel_id=1, source_target_pairs={{1,0},{2,1},{3,2},{4,3},{5,4},{6,5},{7,6},{8,7},{9,8},{10,9},{11,1... | collective-permute-start | bytes 294920 | tf_op jit(solution)/shard_map/while/body/eval_jaxpr/ppermute | solution.py:21
  15.1 8.9 %collective-permute-start.1 = (bf16[64,768]{1,0:T(8,128)(2,1)}, bf16[64,768]{1,0:T(8,128)(2,1)}, u32[]{:S(2)}, u32[]{:S(2)}) collective-permute-start(bf16[64,768]{1,0:T(8,128)(2,1)} %get-tuple-element.579), channel_id=1, source_target_pairs={{0,1},{1,2},{2,3},{3,4},{4,5},{5,6},{6,7},{7,8},{8,9},{9,10},{10,1... | collective-permute-start | bytes 294920 | tf_op jit(solution)/shard_map/while/body/eval_jaxpr/ppermute | solution.py:18
  26.6 7.0 collective-permute-start.2
  27.9 5.7 collective-permute-start.3
  36.1 7.2 collective-permute-start.4
  37.4 6.6 copy-start.8
  38.1 5.3 copy-start.3
  44.0 10.9 %copy-start.7 = (s32[6]{0:T(128)}, s32[6]{0:T(128)S(1)}, u32[]{:S(2)}) copy-start(s32[6]{0:T(128)S(1)} %get-tuple-element.646) | copy-start | bytes 76 | tf_op jit(solution)/shard_map/while
  49.0 9.5 %collective-permute-start = (bf16[64,768]{1,0:T(8,128)(2,1)}, bf16[64,768]{1,0:T(8,128)(2,1)}, u32[]{:S(2)}, u32[]{:S(2)}) collective-permute-start(bf16[64,768]{1,0:T(8,128)(2,1)} %get-tuple-element.578), channel_id=1, source_target_pairs={{1,0},{2,1},{3,2},{4,3},{5,4},{6,5},{7,6},{8,7},{9,8},{10,9},{11,1... | collective-permute-start | bytes 294920 | tf_op jit(solution)/shard_map/while/body/eval_jaxpr/ppermute | solution.py:21
  50.3 8.2 %collective-permute-start.1 = (bf16[64,768]{1,0:T(8,128)(2,1)}, bf16[64,768]{1,0:T(8,128)(2,1)}, u32[]{:S(2)}, u32[]{:S(2)}) collective-permute-start(bf16[64,768]{1,0:T(8,128)(2,1)} %get-tuple-element.579), channel_id=1, source_target_pairs={{0,1},{1,2},{2,3},{3,4},{4,5},{5,6},{6,7},{7,8},{8,9},{9,10},{10,1... | collective-permute-start | bytes 294920 | tf_op jit(solution)/shard_map/while/body/eval_jaxpr/ppermute | solution.py:18
  61.1 7.0 collective-permute-start.2
  62.4 5.7 collective-permute-start.3
  70.7 7.4 collective-permute-start.4
  72.0 6.7 copy-start.8
  72.6 5.4 copy-start.3
  78.7 11.7 %copy-start.7 = (s32[6]{0:T(128)}, s32[6]{0:T(128)S(1)}, u32[]{:S(2)}) copy-start(s32[6]{0:T(128)S(1)} %get-tuple-element.646) | copy-start | bytes 76 | tf_op jit(solution)/shard_map/while
  83.7 10.2 %collective-permute-start = (bf16[64,768]{1,0:T(8,128)(2,1)}, bf16[64,768]{1,0:T(8,128)(2,1)}, u32[]{:S(2)}, u32[]{:S(2)}) collective-permute-start(bf16[64,768]{1,0:T(8,128)(2,1)} %get-tuple-element.578), channel_id=1, source_target_pairs={{1,0},{2,1},{3,2},{4,3},{5,4},{6,5},{7,6},{8,7},{9,8},{10,9},{11,1... | collective-permute-start | bytes 294920 | tf_op jit(solution)/shard_map/while/body/eval_jaxpr/ppermute | solution.py:21
  85.0 8.9 %collective-permute-start.1 = (bf16[64,768]{1,0:T(8,128)(2,1)}, bf16[64,768]{1,0:T(8,128)(2,1)}, u32[]{:S(2)}, u32[]{:S(2)}) collective-permute-start(bf16[64,768]{1,0:T(8,128)(2,1)} %get-tuple-element.579), channel_id=1, source_target_pairs={{0,1},{1,2},{2,3},{3,4},{4,5},{5,6},{6,7},{7,8},{8,9},{9,10},{10,1... | collective-permute-start | bytes 294920 | tf_op jit(solution)/shard_map/while/body/eval_jaxpr/ppermute | solution.py:18
  96.5 7.6 collective-permute-start.2
  97.8 6.3 collective-permute-start.3
  106.7 6.4 collective-permute-start.4
  108.0 5.8 copy-start.8
  113.8 12.2 %copy-start.7 = (s32[6]{0:T(128)}, s32[6]{0:T(128)S(1)}, u32[]{:S(2)}) copy-start(s32[6]{0:T(128)S(1)} %get-tuple-element.646) | copy-start | bytes 76 | tf_op jit(solution)/shard_map/while
  118.8 10.7 %collective-permute-start = (bf16[64,768]{1,0:T(8,128)(2,1)}, bf16[64,768]{1,0:T(8,128)(2,1)}, u32[]{:S(2)}, u32[]{:S(2)}) collective-permute-start(bf16[64,768]{1,0:T(8,128)(2,1)} %get-tuple-element.578), channel_id=1, source_target_pairs={{1,0},{2,1},{3,2},{4,3},{5,4},{6,5},{7,6},{8,7},{9,8},{10,9},{11,1... | collective-permute-start | bytes 294920 | tf_op jit(solution)/shard_map/while/body/eval_jaxpr/ppermute | solution.py:21
  120.1 9.4 %collective-permute-start.1 = (bf16[64,768]{1,0:T(8,128)(2,1)}, bf16[64,768]{1,0:T(8,128)(2,1)}, u32[]{:S(2)}, u32[]{:S(2)}) collective-permute-start(bf16[64,768]{1,0:T(8,128)(2,1)} %get-tuple-element.579), channel_id=1, source_target_pairs={{0,1},{1,2},{2,3},{3,4},{4,5},{5,6},{6,7},{7,8},{8,9},{9,10},{10,1... | collective-permute-start | bytes 294920 | tf_op jit(solution)/shard_map/while/body/eval_jaxpr/ppermute | solution.py:18
  132.1 7.6 collective-permute-start.2
  133.4 6.3 collective-permute-start.3
  142.3 7.5 collective-permute-start.4
  143.6 6.8 copy-start.8
  144.2 5.5 copy-start.3
  150.4 13.7 %copy-start.7 = (s32[6]{0:T(128)}, s32[6]{0:T(128)S(1)}, u32[]{:S(2)}) copy-start(s32[6]{0:T(128)S(1)} %get-tuple-element.646) | copy-start | bytes 76 | tf_op jit(solution)/shard_map/while
  155.4 12.3 %collective-permute-start = (bf16[64,768]{1,0:T(8,128)(2,1)}, bf16[64,768]{1,0:T(8,128)(2,1)}, u32[]{:S(2)}, u32[]{:S(2)}) collective-permute-start(bf16[64,768]{1,0:T(8,128)(2,1)} %get-tuple-element.578), channel_id=1, source_target_pairs={{1,0},{2,1},{3,2},{4,3},{5,4},{6,5},{7,6},{8,7},{9,8},{10,9},{11,1... | collective-permute-start | bytes 294920 | tf_op jit(solution)/shard_map/while/body/eval_jaxpr/ppermute | solution.py:21
  156.7 11.0 %collective-permute-start.1 = (bf16[64,768]{1,0:T(8,128)(2,1)}, bf16[64,768]{1,0:T(8,128)(2,1)}, u32[]{:S(2)}, u32[]{:S(2)}) collective-permute-start(bf16[64,768]{1,0:T(8,128)(2,1)} %get-tuple-element.579), channel_id=1, source_target_pairs={{0,1},{1,2},{2,3},{3,4},{4,5},{5,6},{6,7},{7,8},{8,9},{9,10},{10,1... | collective-permute-start | bytes 294920 | tf_op jit(solution)/shard_map/while/body/eval_jaxpr/ppermute | solution.py:18
  170.3 12.4 %collective-permute-start.2 = (bf16[64,384]{1,0:T(8,128)(2,1)S(1)}, bf16[64,384]{1,0:T(8,128)(2,1)S(1)}, u32[]{:S(2)}, u32[]{:S(2)}) collective-permute-start(bf16[64,384]{1,0:T(8,128)(2,1)S(1)} %get-tuple-element.582), channel_id=1, source_target_pairs={{1,0},{2,1},{3,2},{4,3},{5,4},{6,5},{7,6},{8,7},{9,8},{10,9},{11,1... | collective-permute-start | bytes 147464 | tf_op jit(solution)/shard_map/while/body/eval_jaxpr/ppermute | solution.py:21
  171.6 11.1 %collective-permute-start.3 = (bf16[64,384]{1,0:T(8,128)(2,1)S(1)}, bf16[64,384]{1,0:T(8,128)(2,1)S(1)}, u32[]{:S(2)}, u32[]{:S(2)}) collective-permute-start(bf16[64,384]{1,0:T(8,128)(2,1)S(1)} %get-tuple-element.583), channel_id=1, source_target_pairs={{0,1},{1,2},{2,3},{3,4},{4,5},{5,6},{6,7},{7,8},{8,9},{9,10},{10,1... | collective-permute-start | bytes 147464 | tf_op jit(solution)/shard_map/while/body/eval_jaxpr/ppermute | solution.py:18
  185.3 6.4 collective-permute-start.4
  186.6 5.8 copy-start.8
  192.3 17.0 %copy-start.7 = (s32[6]{0:T(128)}, s32[6]{0:T(128)S(1)}, u32[]{:S(2)}) copy-start(s32[6]{0:T(128)S(1)} %get-tuple-element.646) | copy-start | bytes 76 | tf_op jit(solution)/shard_map/while
  197.4 15.5 %collective-permute-start = (bf16[64,768]{1,0:T(8,128)(2,1)}, bf16[64,768]{1,0:T(8,128)(2,1)}, u32[]{:S(2)}, u32[]{:S(2)}) collective-permute-start(bf16[64,768]{1,0:T(8,128)(2,1)} %get-tuple-element.578), channel_id=1, source_target_pairs={{1,0},{2,1},{3,2},{4,3},{5,4},{6,5},{7,6},{8,7},{9,8},{10,9},{11,1... | collective-permute-start | bytes 294920 | tf_op jit(solution)/shard_map/while/body/eval_jaxpr/ppermute | solution.py:21
  198.7 14.2 %collective-permute-start.1 = (bf16[64,768]{1,0:T(8,128)(2,1)}, bf16[64,768]{1,0:T(8,128)(2,1)}, u32[]{:S(2)}, u32[]{:S(2)}) collective-permute-start(bf16[64,768]{1,0:T(8,128)(2,1)} %get-tuple-element.579), channel_id=1, source_target_pairs={{0,1},{1,2},{2,3},{3,4},{4,5},{5,6},{6,7},{7,8},{8,9},{9,10},{10,1... | collective-permute-start | bytes 294920 | tf_op jit(solution)/shard_map/while/body/eval_jaxpr/ppermute | solution.py:18
  215.4 12.6 %collective-permute-start.2 = (bf16[64,384]{1,0:T(8,128)(2,1)S(1)}, bf16[64,384]{1,0:T(8,128)(2,1)S(1)}, u32[]{:S(2)}, u32[]{:S(2)}) collective-permute-start(bf16[64,384]{1,0:T(8,128)(2,1)S(1)} %get-tuple-element.582), channel_id=1, source_target_pairs={{1,0},{2,1},{3,2},{4,3},{5,4},{6,5},{7,6},{8,7},{9,8},{10,9},{11,1... | collective-permute-start | bytes 147464 | tf_op jit(solution)/shard_map/while/body/eval_jaxpr/ppermute | solution.py:21
  216.7 11.3 %collective-permute-start.3 = (bf16[64,384]{1,0:T(8,128)(2,1)S(1)}, bf16[64,384]{1,0:T(8,128)(2,1)S(1)}, u32[]{:S(2)}, u32[]{:S(2)}) collective-permute-start(bf16[64,384]{1,0:T(8,128)(2,1)S(1)} %get-tuple-element.583), channel_id=1, source_target_pairs={{0,1},{1,2},{2,3},{3,4},{4,5},{5,6},{6,7},{7,8},{8,9},{9,10},{10,1... | collective-permute-start | bytes 147464 | tf_op jit(solution)/shard_map/while/body/eval_jaxpr/ppermute | solution.py:18
  230.7 6.6 collective-permute-start.4
  232.0 5.9 copy-start.8
  240.3 465.3 %reduce-scatter.3.cloned.1.call-start = ((), (), s32[]{:S(2)}) async-start(), calls=%async_computation.2 | async-start | bytes 1880064 | tf_op jit(solution)/shard_map/reduce_scatter | solution.py:149
  241.8 534.8 %all-reduce.2.cloned.1.call-start = ((), (), s32[]{:S(2)}) async-start(), calls=%async_computation.3 | async-start | bytes 221184 | tf_op jit(solution)/shard_map/psum | solution.py:157
  (39 other events, 90.6 us)
Sparse Core Ops, SparseCore 0:
  240.4 254.6 reduce-scatter.4
  500.3 205.1 reduce-scatter.2
  707.9 68.7 all-reduce.1
where the time goes:
time: 787 us; the launch traced here: 785 us
  waiting for transfers between devices  536 us (68%)
  starting transfers between devices  98.7 us (13%)
  other arithmetic  40.7 us (5%)
  matrix products  33.5 us (4%)
  local copies, waits for them, and re-layouts  29.3 us (4%)
  blocking collectives  27.9 us (4%)
  between operations  13.8 us (2%)
    reduce_scatter x1, waiting for transfers between devices, on_device(): lax.psum_scatter(acc_out.astype(jnp.bfloat16), 'seq', scatter_dimension=1...  253 us
    reduce_scatter x1, waiting for transfers between devices, on_device(): lax.psum_scatter(conv_part.astype(jnp.bfloat16), 'seq', scatter_dimension...  183 us
    ppermute x12, starting transfers between devices, with_halo(): lax.ppermute(lax.slice_in_dim(block, block.shape[dim] - width, None, axis...  75.4 us
    psum x1, waiting for transfers between devices, on_device(): lax.psum(shares[0].astype(jnp.bfloat16), 'dp').astype(jnp.float32)  70.4 us
    ppermute x6, waiting for transfers between devices, shifted(): return lax.ppermute(value, axis, pairs)  29.8 us
    psum x1, blocking collectives, on_device(): lax.psum(shares[1].astype(jnp.bfloat16), 'dp').astype(jnp.float32)  27.9 us
  transfers between devices with their start and end apart: 33, of which 9 were waited for; matrix products, arithmetic and copies ran while one was open for 5% of the time, Pallas kernels for 0%

commit v1 on v0

v1 whole, which is shorter than its diff:
```python
import functools

import jax
import jax.numpy as jnp
from jax import lax
from jax.experimental import pallas as pl
from jax.experimental.pallas import tpu as pltpu
from jax.sharding import PartitionSpec as P

BASE_DILATION = 32
MARGIN = 2 * BASE_DILATION
GELU = 0.7978845608028654
CUBIC = 0.044715
MESH = pl.DeviceIdType.MESH
F32 = jnp.float32
BF16 = jnp.bfloat16
NT = (((1,), (1,)), ((), ()))
TN = (((0,), (0,)), ((), ()))


def gelu_pair(z):
    square = z * z
    t = jnp.tanh(z * (GELU + (GELU * CUBIC) * square))
    half = 0.5 + 0.5 * t
    value = z * half
    slope = half + (0.5 * z) * (1.0 - t * t) * (GELU + (3.0 * GELU * CUBIC) * square)
    return value, slope


def y_offsets(ny):
    offsets = [0]
    for dist in range(1, ny // 2 + 1):
        offsets = ([dist] if 2 * dist == ny else [dist, -dist]) + offsets
    return offsets


def kernel(
    sizes,
    x_ref,
    cot_ref,
    cw_ref,
    ow_ref,
    ns_ref,
    nb_ref,
    is_ref,
    ib_ref,
    gin_ref,
    gconv_ref,
    gout_ref,
    hid,
    gcv,
    slope_one,
    slope_two,
    inner,
    act,
    gtop,
    acc,
    part,
    core_in,
    chip,
    xa,
    xb,
    xc,
    row,
    yin,
    col,
    zin,
    final,
    hid_send,
    hid_recv,
    gcv_send,
    gcv_recv,
    sec_send,
    sec_recv,
    core_send,
    core_recv,
    x_send,
    x_recv,
    y_send,
    y_recv,
    z_send,
    z_recv,
    all_send,
    all_recv,
):
    nx, ny, sections = sizes
    micros, rows, channels = x_ref.shape
    width = cw_ref.shape[2]
    block = channels // (2 * ny)
    half_c = channels // 2
    dp = lax.axis_index("dp")
    sec = lax.axis_index("section")
    seq = lax.axis_index("seq")
    x, core = dp // 2, dp % 2
    zh, y = seq // ny, seq % ny
    seqs = 2 * ny
    own = slice(MARGIN, MARGIN + rows)
    parity = sec % 2
    dil = BASE_DILATION * (1 + parity)
    has_prev, has_next = seq > 0, seq < seqs - 1
    is_top = sec == sections - 1

    def device(dp_at=dp, sec_at=sec, seq_at=seq):
        return (dp_at, sec_at, seq_at)

    def remote(src, dst, send, recv, to):
        return pltpu.make_async_remote_copy(
            src_ref=src,
            dst_ref=dst,
            send_sem=send,
            recv_sem=recv,
            device_id=to,
            device_id_type=MESH,
        )

    barrier = pltpu.get_barrier_semaphore()

    def greet(to):
        pl.semaphore_signal(barrier, inc=1, device_id=to, device_id_type=MESH)

    def when_prev(body):
        pl.when(has_prev)(body)

    def when_next(body):
        pl.when(has_next)(body)

    for step in range(1, 2 * nx):
        greet(device(dp_at=lax.rem(dp + step, 2 * nx)))
    for step in range(1, ny):
        greet(device(seq_at=zh * ny + lax.rem(y + step, ny)))
    greet(device(seq_at=(1 - zh) * ny + y))
    crosses_up = jnp.logical_and(zh == 0, y == ny - 1)
    crosses_down = jnp.logical_and(zh == 1, y == 0)
    pl.when(crosses_up)(lambda: greet(device(seq_at=seq + 1)))
    pl.when(crosses_down)(lambda: greet(device(seq_at=seq - 1)))
    pl.when(sec > 0)(lambda: greet(device(sec_at=sec - 1)))
    pl.when(sec < sections - 1)(lambda: greet(device(sec_at=sec + 1)))
    expected = (
        2 * nx - 1 + ny - 1 + 1
        + jnp.where(crosses_up, 1, 0)
        + jnp.where(crosses_down, 1, 0)
        + jnp.where(sec > 0, 1, 0)
        + jnp.where(sec < sections - 1, 1, 0)
    )
    pl.semaphore_wait(barrier, expected)

    def halo(buffer, m, send, recv, step):
        for par in range(2):
            d = BASE_DILATION * (1 + par)

            @pl.when(parity == par)
            def _():
                def up():
                    return remote(
                        buffer.at[m, pl.ds(MARGIN + rows - d, d)],
                        buffer.at[m, pl.ds(MARGIN - d, d)],
                        send.at[m, 0],
                        recv.at[m, 0],
                        device(seq_at=lax.rem(seq + 1, seqs)),
                    )

                def down():
                    return remote(
                        buffer.at[m, pl.ds(MARGIN, d)],
                        buffer.at[m, pl.ds(MARGIN + rows, d)],
                        send.at[m, 1],
                        recv.at[m, 1],
                        device(seq_at=lax.rem(seq + seqs - 1, seqs)),
                    )

                if step == "start":
                    when_next(lambda: up().start())
                    when_prev(lambda: down().start())
                elif step == "recv":
                    when_prev(lambda: up().wait_recv())
                    when_next(lambda: down().wait_recv())
                else:
                    when_next(lambda: up().wait_send())
                    when_prev(lambda: down().wait_send())

    def clear_edges():
        for buffer in (hid, gcv):
            zero = jnp.zeros((micros, MARGIN, buffer.shape[2]), BF16)

            @pl.when(seq == 0)
            def _():
                buffer[:, :MARGIN] = zero

            @pl.when(seq == seqs - 1)
            def _():
                buffer[:, MARGIN + rows :] = zero

    clear_edges()
    tile = 16

    for m in range(micros):

        def activate(i, carry):
            at = pl.multiple_of(i * tile, tile)
            pre = x_ref[m, pl.ds(at, tile), :].astype(F32) * ns_ref[...] + nb_ref[...]
            value, slope = gelu_pair(pre)
            hid[m, pl.ds(MARGIN + at, tile), :] = value.astype(BF16)
            slope_one[m, pl.ds(at, tile), :] = slope * ns_ref[...]
            return carry

        lax.fori_loop(0, rows // tile, activate, 0)
        halo(hid, m, hid_send, hid_recv, "start")

    @pl.when(is_top)
    def _():
        gtop[...] = cot_ref[...]

    def tap_start(k, sign):
        return pl.multiple_of(MARGIN + sign * (k - 1) * dil, BASE_DILATION)

    for m in range(micros):
        halo(hid, m, hid_send, hid_recv, "recv")
        total = None
        for k in range(3):
            term = jnp.dot(
                hid[m, pl.ds(tap_start(k, 1), rows), :], cw_ref[k], preferred_element_type=F32
            )
            total = term if total is None else total + term
        inner[...] = total

        def activate_inner(i, carry):
            at = pl.multiple_of(i * tile, tile)
            pre = inner[pl.ds(at, tile), :] * is_ref[...] + ib_ref[...]
            value, slope = gelu_pair(pre)
            act[m, pl.ds(at, tile), :] = value.astype(BF16)
            slope_two[m, pl.ds(at, tile), :] = slope * is_ref[...]
            return carry

        lax.fori_loop(0, rows // tile, activate_inner, 0)

    pieces = 3
    piece = channels // pieces

    def handed(m, n):
        cut = pl.ds(n * piece, piece)
        return remote(
            gin_ref.at[m, :, cut],
            gtop.at[m, :, cut],
            sec_send.at[m, n],
            sec_recv.at[m, n],
            device(sec_at=lax.rem(sec + sections - 1, sections)),
        )

    def input_grad(m):
        halo(gcv, m, gcv_send, gcv_recv, "recv")
        for n in range(pieces):
            cut = slice(n * piece, (n + 1) * piece)
            total = None
            for k in range(3):
                term = lax.dot_general(
                    gcv[m, pl.ds(tap_start(k, -1), rows), :],
                    cw_ref[k, cut, :],
                    NT,
                    preferred_element_type=F32,
                )
                total = term if total is None else total + term
            gin_ref[m, :, cut] = (
                gtop[m, :, cut].astype(F32) + total * slope_one[m, :, cut]
            ).astype(BF16)
            pl.when(sec > 0)(lambda: handed(m, n).start())

    def weight_grad(m, side):
        cut = pl.ds(pl.multiple_of(side * half_c, 128), half_c)
        for k in range(4):
            if k < 3:
                lhs = hid[m, pl.ds(tap_start(k, 1), rows), cut]
                rhs = gcv[m, own, :]
            else:
                lhs = gtop[m, :, cut]
                rhs = act[m]
            term = lax.dot_general(lhs, rhs, TN, preferred_element_type=F32)
            if m > 0:
                term = term + acc[side, k]
            if m < micros - 1:
                acc[side, k] = term
            else:
                part[side, :, k] = term.reshape(ny, block, width).astype(BF16)

    offsets = y_offsets(ny)
    chunk_y = [lax.rem(y + off + ny, ny) for off in offsets]
    chunks = len(offsets)

    def core_copy(j):
        return remote(
            part.at[1 - core, chunk_y[j]],
            core_in.at[j],
            core_send.at[j],
            core_recv.at[j],
            device(dp_at=dp + 1 - 2 * core),
        )

    for m in range(micros):

        @pl.when(jnp.logical_not(is_top))
        def _():
            for n in range(pieces):
                handed(m, n).wait_recv()

        grad_inner = lax.dot_general(gtop[m], ow_ref[...], NT, preferred_element_type=F32)
        gcv[m, own, :] = (grad_inner * slope_two[m]).astype(BF16)
        halo(gcv, m, gcv_send, gcv_recv, "start")
        weight_grad(m, 1 - core)
        if m == micros - 1:
            for j in range(chunks):
                core_copy(j).start()
        weight_grad(m, core)
        if m < micros - 1:
            input_grad(m)
        else:
            pl.when(sec > 0)(lambda: input_grad(m))

    def x_device(step):
        return device(dp_at=lax.rem(x + step + nx, nx) * 2 + core)

    def x_sign(j):
        return 1 if j % 2 == 0 else -1

    def x_at(step):
        return lax.rem(x + step + nx, nx)

    def x_far(j):
        sign = x_sign(j)
        return remote(
            chip.at[j, x_at(2)], xa.at[j], x_send.at[j, 0], x_recv.at[j, 0], x_device(sign)
        )

    def x_back(j):
        sign = x_sign(j)
        return remote(
            chip.at[j, x_at(-sign)], xb.at[j], x_send.at[j, 1], x_recv.at[j, 1], x_device(-sign)
        )

    def x_ahead(j):
        sign = x_sign(j)
        return remote(
            chip.at[j, x_at(sign)], xc.at[j], x_send.at[j, 2], x_recv.at[j, 2], x_device(sign)
        )

    def y_copy(j):
        return remote(
            row.at[j], yin.at[j], y_send.at[j], y_recv.at[j], device(seq_at=zh * ny + chunk_y[j])
        )

    def stage_core(j):
        core_copy(j).wait_recv()
        chip[j] = (part[core, chunk_y[j]].astype(F32) + core_in[j].astype(F32)).astype(BF16)
        x_far(j).start()
        x_back(j).start()

    def stage_x(j):
        ahead = x_at(x_sign(j))
        x_far(j).wait_recv()
        chip[j, ahead] = (chip[j, ahead].astype(F32) + xa[j].astype(F32)).astype(BF16)
        x_ahead(j).start()

    def stage_y(j):
        x_back(j).wait_recv()
        x_ahead(j).wait_recv()
        total = chip[j, x].astype(F32) + xb[j].astype(F32) + xc[j].astype(F32)
        row[j] = total.astype(BF16)
        if offsets[j] != 0:
            y_copy(j).start()

    lag = 2
    for j in range(chunks + 2 * lag):
        if j < chunks:
            stage_core(j)
        if 0 <= j - lag < chunks:
            stage_x(j - lag)
        if 0 <= j - 2 * lag < chunks:
            stage_y(j - 2 * lag)

    pl.when(sec == 0)(lambda: input_grad(micros - 1))

    total = row[chunks - 1].astype(F32)
    for j in range(chunks - 1):
        y_copy(j).wait_recv()
        total = total + yin[j].astype(F32)
    col[...] = total.astype(BF16)

    def z_copy():
        return remote(col, zin, z_send.at[0], z_recv.at[0], device(seq_at=(1 - zh) * ny + y))

    def spread(step):
        return remote(
            final.at[x],
            final.at[x],
            all_send.at[step],
            all_recv.at[x],
            device(dp_at=lax.rem(dp + step, 2 * nx)),
        )

    def arrival(k):
        return remote(final.at[k], final.at[k], all_send.at[0], all_recv.at[k], device())

    keeps = core == zh
    order = sorted(range(1, 2 * nx), key=lambda s: -min(s, 2 * nx - s))

    @pl.when(jnp.logical_not(keeps))
    def _():
        z_copy().start()

    @pl.when(keeps)
    def _():
        z_copy().wait_recv()
        final[x] = (col[...].astype(F32) + zin[...].astype(F32)).astype(BF16)
        for step in order:
            spread(step).start()

    for k in range(4):
        pl.when(jnp.logical_or(jnp.logical_not(keeps), x != k))(lambda: arrival(k).wait_recv())

    factor = 1.0 / float(micros * 2 * nx)
    for k in range(3):
        gconv_ref[k] = final[k].astype(F32) * factor
    gout_ref[...] = final[3].astype(F32) * factor

    for m in range(micros):
        halo(hid, m, hid_send, hid_recv, "send")
        halo(gcv, m, gcv_send, gcv_recv, "send")

        @pl.when(sec > 0)
        def _():
            for n in range(pieces):
                handed(m, n).wait_send()

    for j in range(chunks):
        core_copy(j).wait_send()
        x_far(j).wait_send()
        x_back(j).wait_send()
        x_ahead(j).wait_send()
        if offsets[j] != 0:
            y_copy(j).wait_send()

    @pl.when(jnp.logical_not(keeps))
    def _():
        z_copy().wait_send()

    @pl.when(keeps)
    def _():
        for step in order:
            spread(step).wait_send()


def on_device(
    sizes,
    section_inputs,
    cotangent,
    conv_weight,
    out_weight,
    norm_scale,
    norm_shift,
    inner_scale,
    inner_shift,
):
    nx, ny, sections = sizes
    inputs = section_inputs[0, :, 0]
    micros, rows, channels = inputs.shape
    width = conv_weight.shape[3]
    block = channels // (2 * ny)
    padded = rows + 2 * MARGIN
    dma = pltpu.SemaphoreType.DMA
    vmem = pl.BlockSpec(memory_space=pltpu.VMEM)
    half_c = channels // 2
    grad_in, grad_conv, grad_out = pl.pallas_call(
        functools.partial(kernel, sizes),
        name="tower_backward",
        out_shape=(
            jax.ShapeDtypeStruct((micros, rows, channels), BF16),
            jax.ShapeDtypeStruct((3, block, width), F32),
            jax.ShapeDtypeStruct((block, width), F32),
        ),
        in_specs=[vmem] * 8,
        out_specs=(vmem,) * 3,
        scratch_shapes=[
            pltpu.VMEM((micros, padded, channels), BF16),
            pltpu.VMEM((micros, padded, width), BF16),
            pltpu.VMEM((micros, rows, channels), F32),
            pltpu.VMEM((micros, rows, width), F32),
            pltpu.VMEM((rows, width), F32),
            pltpu.VMEM((micros, rows, width), BF16),
            pltpu.VMEM((micros, rows, channels), BF16),
            pltpu.VMEM((2, 4, half_c, width), F32),
            pltpu.VMEM((2, ny, 4, block, width), BF16),
            pltpu.VMEM((ny, 4, block, width), BF16),
            pltpu.VMEM((ny, 4, block, width), BF16),
            pltpu.VMEM((ny, block, width), BF16),
            pltpu.VMEM((ny, block, width), BF16),
            pltpu.VMEM((ny, block, width), BF16),
            pltpu.VMEM((ny, block, width), BF16),
            pltpu.VMEM((ny, block, width), BF16),
            pltpu.VMEM((block, width), BF16),
            pltpu.VMEM((block, width), BF16),
            pltpu.VMEM((4, block, width), BF16),
            dma((micros, 2)),
            dma((micros, 2)),
            dma((micros, 2)),
            dma((micros, 2)),
            dma((micros, 3)),
            dma((micros, 3)),
            dma((ny,)),
            dma((ny,)),
            dma((ny, 3)),
            dma((ny, 3)),
            dma((ny,)),
            dma((ny,)),
            dma((1,)),
            dma((1,)),
            dma((2 * nx,)),
            dma((4,)),
        ],
        compiler_params=pltpu.CompilerParams(
            collective_id=0, has_side_effects=True, vmem_limit_bytes=56 * 1024 * 1024
        ),
    )(
        inputs,
        cotangent[:, 0],
        conv_weight[0],
        out_weight[0],
        norm_scale,
        norm_shift,
        inner_scale,
        inner_shift,
    )
    return (
        grad_in.reshape(section_inputs.shape),
        grad_conv[None],
        grad_out.T[None],
    )


def solution(mesh):
    sizes = (mesh.shape["dp"] // 2, mesh.shape["seq"] // 2, mesh.shape["section"])
    return jax.shard_map(
        functools.partial(on_device, sizes),
        mesh=mesh,
        in_specs=(
            P("section", None, "dp", "seq", None),
            P(None, "dp", "seq", None),
            P("section", None, None, None),
            P("section", None, None),
            P("section", None),
            P("section", None),
            P("section", None),
            P("section", None),
        ),
        out_specs=(
            P("section", None, "dp", "seq", None),
            P("section", None, "seq", None),
            P("section", None, "seq"),
        ),
        check_vma=False,
    )
```

time: 787 us -> 126 us (0.16)
  waiting for transfers between devices: 536 us -> 0 us
  Pallas kernels: 0 us -> 120 us
  starting transfers between devices: 98.7 us -> 0 us
  other arithmetic: 40.7 us -> 0 us
  matrix products: 33.5 us -> 0 us
  blocking collectives: 27.9 us -> 0 us
  local copies, waits for them, and re-layouts: 29.3 us -> 5.07 us
  between operations: 13.8 us -> 0.64 us
    reduce_scatter x2 -> x0, waiting for transfers between devices: 436 us -> none  [the longest x1 253 us: on_device(): lax.psum_scatter(acc_out.astype(jnp.bfloat16), 'seq', scatter_dimension=1...]
    pallas_call x0 -> x1, Pallas kernels: none -> 120 us  [on_device(): pl.pallas_call(functools.partial(kernel, sizes), name='tower_backward', o...]
    ppermute x30 -> x0, starting transfers between devices: 98.5 us -> none  [the longest x12 75.4 us: with_halo(): lax.ppermute(lax.slice_in_dim(block, block.shape[dim] - width, None, axis...]
    psum x1 -> x0, waiting for transfers between devices: 70.4 us -> none  [on_device(): lax.psum(shares[0].astype(jnp.bfloat16), 'dp').astype(jnp.float32)]
    dot_general x30 -> x0, matrix products: 33.5 us -> none  [the longest x6 15 us: tick(): lax.dot_general(back_taps, convolution_kernel, (((1, 2), (0, 2)), ((), ()...]
    ppermute x30 -> x0, waiting for transfers between devices: 29.8 us -> none  [the longest x6 29.8 us: shifted(): return lax.ppermute(value, axis, pairs)]
    psum x1 -> x0, blocking collectives: 27.9 us -> none  [on_device(): lax.psum(shares[1].astype(jnp.bfloat16), 'dp').astype(jnp.float32)]
    while x109 -> x0, local copies, waits for them, and re-layouts: 14 us -> none
  transfers between devices with their start and end apart: 33 -> 0, of which waited for: 9 -> 0; matrix products, arithmetic and copies ran while one was open for 5% -> 0% of each run, Pallas kernels for 0% -> 0%
where the time goes in v1:
time: 126 us
  Pallas kernels  120 us (95%)
  local copies, waits for them, and re-layouts  5.07 us (4%)
    pallas_call x1, Pallas kernels, on_device(): pl.pallas_call(functools.partial(kernel, sizes), name='tower_backward', o...  120 us
    unnamed x3, local copies, waits for them, and re-layouts  5.07 us

profile of v1, /device:TPU:1, one launch (start us, length us, event | category | flops | bytes accessed | tf_op | source)
XLA Modules:
  0.0 125.6 jit_solution(16462512875885653367)
XLA Ops:
  0.6 119.9 %tower_backward.1 = (bf16[3,128,768]{2,1,0:T(8,128)(2,1)}, f32[3,48,384]{2,1,0:T(8,128)}, f32[48,384]{1,0:T(8,128)}) custom-call(bf16[3,128,768]{2,1,0:T(8,128)(2,1)} %bitcast.13, bf16[3,128,768]{2,1,0:T(8,128)(2,1)} %bitcast.14, bf16[3,768,384]{2,1,0:T(8,128)(2,1)} %bitcast.11, bf16[384,768]{1,0:T(8,128)(2,1)} %bitcast.15, f32[1,768]{1,0:T(1,128)} %ns_ref.1, ...), custom_call_target="tpu_custom_call" | custom-call | tf_op jit(solution)/shard_map/tower_backward/pallas_call | solution.py:470
  120.5 1.9 %copy.15 = bf16[1,3,1,128,768]{4,3,2,1,0:T(8,128)(2,1)} copy(bf16[1,3,1,128,768]{4,3,2,1,0:T(8,128)(2,1)} %bitcast.12) | data formatting | bytes 1179648
  122.4 1.6 %copy.16 = f32[1,3,48,384]{3,2,1,0:T(8,128)} copy(f32[1,3,48,384]{3,2,1,0:T(8,128)} %bitcast.16) | data formatting | bytes 442368
  124.1 1.5 %copy.17 = f32[1,384,48]{1,2,0:T(8,128)} copy(f32[1,384,48]{1,2,0:T(8,128)} %bitcast.17) | data formatting | bytes 147456

commit v2 on v1

v2 whole, which is shorter than its diff:
```python
import functools

import jax
import jax.numpy as jnp
from jax import lax
from jax.experimental import pallas as pl
from jax.experimental.pallas import tpu as pltpu
from jax.sharding import PartitionSpec as P

BASE_DILATION = 32
MARGIN = 2 * BASE_DILATION
GELU = 0.7978845608028654
CUBIC = 0.044715
MESH = pl.DeviceIdType.MESH
F32 = jnp.float32
BF16 = jnp.bfloat16
TN = (((0,), (0,)), ((), ()))


def gelu_pair(z):
    square = z * z
    t = jnp.tanh(z * (GELU + (GELU * CUBIC) * square))
    half = 0.5 + 0.5 * t
    value = z * half
    slope = half + (0.5 * z) * (1.0 - t * t) * (GELU + (3.0 * GELU * CUBIC) * square)
    return value, slope


def kernel(
    sizes,
    x_in,
    cot_in,
    cw_in,
    ow_in,
    ns_in,
    nb_in,
    is_in,
    ib_in,
    gin_ref,
    total_ref,
    x_ref,
    gtop,
    cw_ref,
    ow_ref,
    ns_ref,
    nb_ref,
    is_ref,
    ib_ref,
    cwt,
    owt,
    hid,
    gcv,
    slope_one,
    slope_two,
    inner,
    act,
    lhs,
    rhs,
    acc,
    row,
    yin,
    col,
    zin,
    load_sem,
    hid_send,
    hid_recv,
    gcv_send,
    gcv_recv,
    sec_send,
    sec_recv,
    lhs_send,
    lhs_recv,
    rhs_send,
    rhs_recv,
    y_send,
    y_recv,
    z_send,
    z_recv,
    all_send,
    all_recv,
):
    nx, ny, sections = sizes
    micros, rows, channels = x_ref.shape
    width = cw_ref.shape[2]
    half_c = channels // 2
    block = half_c // ny
    group = 2 * nx
    dp = lax.axis_index("dp")
    sec = lax.axis_index("section")
    seq = lax.axis_index("seq")
    x, core = dp // 2, dp % 2
    zh, y = seq // ny, seq % ny
    seqs = 2 * ny
    own = slice(MARGIN, MARGIN + rows)
    parity = sec % 2
    dil = BASE_DILATION * (1 + parity)
    has_prev, has_next = seq > 0, seq < seqs - 1
    is_top = sec == sections - 1
    not_top = sec < sections - 1
    is_low = sec == 0
    not_low = sec > 0

    def device(dp_at=dp, sec_at=sec, seq_at=seq):
        return (dp_at, sec_at, seq_at)

    def remote(src, dst, send, recv, to):
        return pltpu.make_async_remote_copy(
            src_ref=src,
            dst_ref=dst,
            send_sem=send,
            recv_sem=recv,
            device_id=to,
            device_id_type=MESH,
        )

    barrier = pltpu.get_barrier_semaphore()

    def greet(to):
        pl.semaphore_signal(barrier, inc=1, device_id=to, device_id_type=MESH)

    for step in range(1, group):
        greet(device(dp_at=lax.rem(dp + step, group)))
    for step in range(1, ny):
        greet(device(seq_at=zh * ny + lax.rem(y + step, ny)))
    greet(device(seq_at=(1 - zh) * ny + y))
    crosses_up = jnp.logical_and(zh == 0, y == ny - 1)
    crosses_down = jnp.logical_and(zh == 1, y == 0)
    pl.when(crosses_up)(lambda: greet(device(seq_at=seq + 1)))
    pl.when(crosses_down)(lambda: greet(device(seq_at=seq - 1)))
    pl.when(not_low)(lambda: greet(device(sec_at=sec - 1)))
    pl.when(not_top)(lambda: greet(device(sec_at=sec + 1)))
    expected = (
        group - 1 + ny - 1 + 1
        + jnp.where(crosses_up, 1, 0)
        + jnp.where(crosses_down, 1, 0)
        + jnp.where(not_low, 1, 0)
        + jnp.where(not_top, 1, 0)
    )

    def load(src, dst, i):
        return pltpu.make_async_copy(src, dst, load_sem.at[i])

    small = ((ns_in, ns_ref), (nb_in, nb_ref), (is_in, is_ref), (ib_in, ib_ref))

    def loads_small():
        return [load(src, dst, i) for i, (src, dst) in enumerate(small)]

    def load_x(m):
        return load(x_in.at[m], x_ref.at[m], 4 + m)

    def load_cw():
        return load(cw_in, cw_ref, 7)

    def load_ow():
        return load(ow_in, ow_ref, 8)

    def load_cot():
        return load(cot_in, gtop, 9)

    for copy in loads_small():
        copy.start()
    for m in range(micros):
        load_x(m).start()
    load_cw().start()
    load_ow().start()
    pl.when(is_top)(lambda: load_cot().start())

    def halo(buffer, m, send, recv, step):
        for par in range(2):
            d = BASE_DILATION * (1 + par)

            @pl.when(parity == par)
            def _():
                def up():
                    return remote(
                        buffer.at[m, pl.ds(MARGIN + rows - d, d)],
                        buffer.at[m, pl.ds(MARGIN - d, d)],
                        send.at[m, 0],
                        recv.at[m, 0],
                        device(seq_at=lax.rem(seq + 1, seqs)),
                    )

                def down():
                    return remote(
                        buffer.at[m, pl.ds(MARGIN, d)],
                        buffer.at[m, pl.ds(MARGIN + rows, d)],
                        send.at[m, 1],
                        recv.at[m, 1],
                        device(seq_at=lax.rem(seq + seqs - 1, seqs)),
                    )

                if step == "start":
                    pl.when(has_next)(lambda: up().start())
                    pl.when(has_prev)(lambda: down().start())
                elif step == "recv":
                    pl.when(has_prev)(lambda: up().wait_recv())
                    pl.when(has_next)(lambda: down().wait_recv())
                else:
                    pl.when(has_next)(lambda: up().wait_send())
                    pl.when(has_prev)(lambda: down().wait_send())

    for buffer in (hid, gcv):
        zero = jnp.zeros((micros, MARGIN, buffer.shape[2]), BF16)

        @pl.when(seq == 0)
        def _():
            buffer[:, :MARGIN] = zero

        @pl.when(seq == seqs - 1)
        def _():
            buffer[:, MARGIN + rows :] = zero

    tile = 16
    for copy in loads_small():
        copy.wait()

    for m in range(micros):
        load_x(m).wait()

        def activate(i, carry):
            at = pl.multiple_of(i * tile, tile)
            pre = x_ref[m, pl.ds(at, tile), :].astype(F32) * ns_ref[...] + nb_ref[...]
            value, slope = gelu_pair(pre)
            hid[m, pl.ds(MARGIN + at, tile), :] = value.astype(BF16)
            slope_one[m, pl.ds(at, tile), :] = slope * ns_ref[...]
            return carry

        lax.fori_loop(0, rows // tile, activate, 0)
        if m == 0:
            pl.semaphore_wait(barrier, expected)
        halo(hid, m, hid_send, hid_recv, "start")

    load_ow().wait()
    owt[...] = ow_ref[...].T
    load_cw().wait()
    for k in range(3):
        cwt[k] = cw_ref[k].T
    pl.when(is_top)(lambda: load_cot().wait())

    def tap_start(k, sign):
        return pl.multiple_of(MARGIN + sign * (k - 1) * dil, BASE_DILATION)

    def inner_forward(m):
        halo(hid, m, hid_send, hid_recv, "recv")
        total = None
        for k in range(3):
            term = jnp.dot(
                hid[m, pl.ds(tap_start(k, 1), rows), :], cw_ref[k], preferred_element_type=F32
            )
            total = term if total is None else total + term
        inner[...] = total

        def activate_inner(i, carry):
            at = pl.multiple_of(i * tile, tile)
            pre = inner[pl.ds(at, tile), :] * is_ref[...] + ib_ref[...]
            value, slope = gelu_pair(pre)
            act[m, pl.ds(at, tile), :] = value.astype(BF16)
            slope_two[m, pl.ds(at, tile), :] = slope * is_ref[...]
            return carry

        lax.fori_loop(0, rows // tile, activate_inner, 0)

    pieces = 3
    piece = channels // pieces

    def handed(m, n):
        cut = pl.ds(n * piece, piece)
        return remote(
            gin_ref.at[m, :, cut],
            gtop.at[m, :, cut],
            sec_send.at[m, n],
            sec_recv.at[m, n],
            device(sec_at=lax.rem(sec + sections - 1, sections)),
        )

    def input_grad(m, send):
        halo(gcv, m, gcv_send, gcv_recv, "recv")
        for n in range(pieces):
            cut = slice(n * piece, (n + 1) * piece)
            total = None
            for k in range(3):
                term = jnp.dot(
                    gcv[m, pl.ds(tap_start(k, -1), rows), :],
                    cwt[k, :, cut],
                    preferred_element_type=F32,
                )
                total = term if total is None else total + term
            gin_ref[m, :, cut] = (
                gtop[m, :, cut].astype(F32) + total * slope_one[m, :, cut]
            ).astype(BF16)
            if send:
                handed(m, n).start()

    steps = sorted(range(1, group), key=lambda t: -min(t, group - t))

    def peer(t):
        to = lax.rem(dp + t, group)
        return to, to // 2, lax.rem(to, 2)

    def half(c):
        return pl.ds(pl.multiple_of(c * half_c, 128), half_c)

    def lhs_tap(m, t):
        to, to_x, to_c = peer(t)
        return remote(
            hid.at[m, pl.ds(tap_start(to_x, 1), rows), half(to_c)],
            lhs.at[m, dp],
            lhs_send.at[m, t],
            lhs_recv.at[m, dp],
            device(dp_at=to),
        )

    def lhs_top(m, t):
        to, _, to_c = peer(t)
        return remote(
            gtop.at[m, :, half(to_c)],
            lhs.at[m, dp],
            lhs_send.at[m, t],
            lhs_recv.at[m, dp],
            device(dp_at=to),
        )

    def rhs_conv(m, t):
        to, _, _ = peer(t)
        return remote(
            gcv.at[m, pl.ds(MARGIN, rows)],
            rhs.at[m, dp],
            rhs_send.at[m, t],
            rhs_recv.at[m, dp],
            device(dp_at=to),
        )

    def rhs_act(m, t):
        to, _, _ = peer(t)
        return remote(
            act.at[m],
            rhs.at[m, dp],
            rhs_send.at[m, t],
            rhs_recv.at[m, dp],
            device(dp_at=to),
        )

    def exchange_early(m):
        for t in steps:
            _, to_x, _ = peer(t)
            pl.when(to_x < 3)(lambda: lhs_tap(m, t).start())
            pl.when(to_x == 3)(lambda: rhs_act(m, t).start())

    def exchange_late(m):
        for t in steps:
            _, to_x, _ = peer(t)
            pl.when(to_x < 3)(lambda: rhs_conv(m, t).start())
            pl.when(to_x == 3)(lambda: lhs_top(m, t).start())

    def weight_grad(m):
        @pl.when(x < 3)
        def _():
            lhs[m, dp] = hid[m, pl.ds(tap_start(x, 1), rows), half(core)]
            rhs[m, dp] = gcv[m, own, :]

        @pl.when(x == 3)
        def _():
            lhs[m, dp] = gtop[m, :, half(core)]
            rhs[m, dp] = act[m]

        for t in steps:
            source = lax.rem(dp + t, group)
            arrival = [
                remote(buffer.at[m, source], buffer.at[m, source], send.at[m, t], recv.at[m, source], device())
                for buffer, send, recv in ((lhs, lhs_send, lhs_recv), (rhs, rhs_send, rhs_recv))
            ]
            for copy in arrival:
                copy.wait_recv()
        term = lax.dot_general(
            lhs[m].reshape(group * rows, half_c),
            rhs[m].reshape(group * rows, width),
            TN,
            preferred_element_type=F32,
        )
        if m > 0:
            term = term + acc[...]
        if m < micros - 1:
            acc[...] = term
        else:
            row[...] = term.reshape(ny, block, width).astype(BF16)

    @pl.when(not_top)
    def _():
        for m in range(micros):
            inner_forward(m)
            exchange_early(m)

    for m in range(micros):

        @pl.when(is_top)
        def _():
            inner_forward(m)

        @pl.when(not_top)
        def _():
            for n in range(pieces):
                handed(m, n).wait_recv()

        grad_inner = jnp.dot(gtop[m], owt[...], preferred_element_type=F32)
        gcv[m, own, :] = (grad_inner * slope_two[m]).astype(BF16)
        halo(gcv, m, gcv_send, gcv_recv, "start")
        pl.when(is_top)(lambda: exchange_early(m))
        exchange_late(m)
        if m > 0:
            pl.when(not_low)(lambda: input_grad(m - 1, True))
    pl.when(not_low)(lambda: input_grad(micros - 1, True))

    weight_grad(0)

    @pl.when(is_low)
    def _():
        for m in range(micros - 1):
            input_grad(m, False)

    for m in range(1, micros):
        weight_grad(m)

    def y_copy(t):
        to = lax.rem(y + t, ny)
        return remote(
            row.at[to], yin.at[t], y_send.at[t], y_recv.at[t], device(seq_at=zh * ny + to)
        )

    far_first = sorted(range(1, ny), key=lambda t: -min(t, ny - t))
    for t in far_first:
        y_copy(t).start()

    pl.when(is_low)(lambda: input_grad(micros - 1, False))

    total = row[y].astype(F32)
    for t in reversed(far_first):
        y_copy(t).wait_recv()
        total = total + yin[t].astype(F32)
    col[...] = total.astype(BF16)

    def z_copy():
        return remote(col, zin, z_send.at[0], z_recv.at[0], device(seq_at=(1 - zh) * ny + y))

    def spread(t):
        return remote(
            total_ref.at[x],
            total_ref.at[x],
            all_send.at[t],
            all_recv.at[x],
            device(dp_at=lax.rem(dp + t, group)),
        )

    def arrival_of(k):
        return remote(total_ref.at[k], total_ref.at[k], all_send.at[0], all_recv.at[k], device())

    keeps = core == zh

    @pl.when(jnp.logical_not(keeps))
    def _():
        z_copy().start()

    @pl.when(keeps)
    def _():
        z_copy().wait_recv()
        total_ref[x] = (col[...].astype(F32) + zin[...].astype(F32)).astype(BF16)
        for t in steps:
            spread(t).start()

    for k in range(4):
        pl.when(jnp.logical_or(jnp.logical_not(keeps), x != k))(lambda: arrival_of(k).wait_recv())

    for m in range(micros):
        halo(hid, m, hid_send, hid_recv, "send")
        halo(gcv, m, gcv_send, gcv_recv, "send")

        @pl.when(not_low)
        def _():
            for n in range(pieces):
                handed(m, n).wait_send()

        for t in steps:
            lhs_top(m, t).wait_send()
            rhs_conv(m, t).wait_send()

    for t in far_first:
        y_copy(t).wait_send()

    @pl.when(jnp.logical_not(keeps))
    def _():
        z_copy().wait_send()

    @pl.when(keeps)
    def _():
        for t in steps:
            spread(t).wait_send()


def finish(factor, gin_in, total_in, gin_ref, gconv_ref, gout_ref):
    gin_ref[...] = gin_in[...]
    gconv_ref[...] = total_in[:3].astype(F32) * factor
    gout_ref[...] = total_in[3].astype(F32) * factor


def on_device(
    sizes,
    section_inputs,
    cotangent,
    conv_weight,
    out_weight,
    norm_scale,
    norm_shift,
    inner_scale,
    inner_shift,
):
    nx, ny, sections = sizes
    inputs = section_inputs[0, :, 0]
    micros, rows, channels = inputs.shape
    width = conv_weight.shape[3]
    half_c = channels // 2
    block = half_c // ny
    group = 2 * nx
    padded = rows + 2 * MARGIN
    dma = pltpu.SemaphoreType.DMA
    vmem = pl.BlockSpec(memory_space=pltpu.VMEM)
    anywhere = pl.BlockSpec(memory_space=pl.ANY)
    grad_in, total = pl.pallas_call(
        functools.partial(kernel, sizes),
        name="tower_backward",
        out_shape=(
            jax.ShapeDtypeStruct((micros, rows, channels), BF16),
            jax.ShapeDtypeStruct((4, block, width), BF16),
        ),
        in_specs=[anywhere] * 8,
        out_specs=(vmem, vmem),
        scratch_shapes=[
            pltpu.VMEM((micros, rows, channels), BF16),
            pltpu.VMEM((micros, rows, channels), BF16),
            pltpu.VMEM((3, channels, width), BF16),
            pltpu.VMEM((width, channels), BF16),
            pltpu.VMEM((1, channels), F32),
            pltpu.VMEM((1, channels), F32),
            pltpu.VMEM((1, width), F32),
            pltpu.VMEM((1, width), F32),
            pltpu.VMEM((3, width, channels), BF16),
            pltpu.VMEM((channels, width), BF16),
            pltpu.VMEM((micros, padded, channels), BF16),
            pltpu.VMEM((micros, padded, width), BF16),
            pltpu.VMEM((micros, rows, channels), F32),
            pltpu.VMEM((micros, rows, width), F32),
            pltpu.VMEM((rows, width), F32),
            pltpu.VMEM((micros, rows, width), BF16),
            pltpu.VMEM((micros, group, rows, half_c), BF16),
            pltpu.VMEM((micros, group, rows, width), BF16),
            pltpu.VMEM((half_c, width), F32),
            pltpu.VMEM((ny, block, width), BF16),
            pltpu.VMEM((ny, block, width), BF16),
            pltpu.VMEM((block, width), BF16),
            pltpu.VMEM((block, width), BF16),
            dma((10,)),
            dma((micros, 2)),
            dma((micros, 2)),
            dma((micros, 2)),
            dma((micros, 2)),
            dma((micros, 3)),
            dma((micros, 3)),
            dma((micros, group)),
            dma((micros, group)),
            dma((micros, group)),
            dma((micros, group)),
            dma((ny,)),
            dma((ny,)),
            dma((1,)),
            dma((1,)),
            dma((group,)),
            dma((4,)),
        ],
        compiler_params=pltpu.CompilerParams(
            collective_id=0, has_side_effects=True, vmem_limit_bytes=56 * 1024 * 1024
        ),
    )(
        inputs,
        cotangent[:, 0],
        conv_weight[0],
        out_weight[0],
        norm_scale,
        norm_shift,
        inner_scale,
        inner_shift,
    )
    grad_in, grad_conv, grad_out = pl.pallas_call(
        functools.partial(finish, 1.0 / float(micros * group)),
        name="write_results",
        out_shape=(
            jax.ShapeDtypeStruct((micros, rows, channels), BF16),
            jax.ShapeDtypeStruct((3, block, width), F32),
            jax.ShapeDtypeStruct((block, width), F32),
        ),
        in_specs=[vmem] * 2,
        out_specs=(vmem,) * 3,
    )(grad_in, total)
    return (
        grad_in.reshape(section_inputs.shape),
        grad_conv[None],
        grad_out.T[None],
    )


def solution(mesh):
    sizes = (mesh.shape["dp"] // 2, mesh.shape["seq"] // 2, mesh.shape["section"])
    return jax.shard_map(
        functools.partial(on_device, sizes),
        mesh=mesh,
        in_specs=(
            P("section", None, "dp", "seq", None),
            P(None, "dp", "seq", None),
            P("section", None, None, None),
            P("section", None, None),
            P("section", None),
            P("section", None),
            P("section", None),
            P("section", None),
        ),
        out_specs=(
            P("section", None, "dp", "seq", None),
            P("section", None, "seq", None),
            P("section", None, "seq"),
        ),
        check_vma=False,
    )
```

time: 126 us -> 104 us (0.83)
  Pallas kernels: 120 us -> 103 us
  local copies, waits for them, and re-layouts: 5.07 us -> 0 us
    pallas_call x1, Pallas kernels: 120 us -> 101 us  [on_device(): pl.pallas_call(functools.partial(kernel, sizes), name='tower_backward', o...]
    unnamed x3 -> x0, local copies, waits for them, and re-layouts: 5.07 us -> none
    pallas_call x0 -> x1, Pallas kernels: none -> 2.01 us  [on_device(): pl.pallas_call(functools.partial(finish, 1.0 / float(micros * group)), na...]
where the time goes in v2:
time: 104 us; the launch traced here: 103 us
  Pallas kernels  103 us (99%)
    pallas_call x1, Pallas kernels, on_device(): pl.pallas_call(functools.partial(kernel, sizes), name='tower_backward', o...  101 us

profile of v2, /device:TPU:1, one launch (start us, length us, event | category | flops | bytes accessed | tf_op | source)
XLA Modules:
  0.0 103.5 jit_solution(556006890207972809)
XLA Ops:
  0.6 100.8 %tower_backward.1 = (bf16[3,128,768]{2,1,0:T(8,128)(2,1)}, bf16[4,48,384]{2,1,0:T(8,128)(2,1)}) custom-call(bf16[3,128,768]{2,1,0:T(8,128)(2,1)} %bitcast.12, bf16[3,128,768]{2,1,0:T(8,128)(2,1)} %bitcast.13, bf16[3,768,384]{2,1,0:T(8,128)(2,1)} %bitcast.11, bf16[384,768]{1,0:T(8,128)(2,1)} %bitcast.14, f32[1,768]{1,0:T(1,128)} %ns_in.1, f32[1,768]{1,0:T(1,128)} %nb_in.1, ...), custom_call_target="tpu_custom_call" | custom-call | tf_op jit(solution)/shard_map/tower_backward/pallas_call | solution.py:526
  101.5 2.0 %write_results.1 = (bf16[3,128,768]{2,1,0:T(8,128)(2,1)}, f32[3,48,384]{2,1,0:T(8,128)}, f32[48,384]{1,0:T(8,128)}) custom-call(bf16[3,128,768]{2,1,0:T(8,128)(2,1)} %get-tuple-element.8.gin_in, bf16[4,48,384]{2,1,0:T(8,128)(2,1)} %get-tuple-element.9.total_in), custom_call_target="tpu_custom_call" | custom-call | tf_op jit(solution)/shard_map/write_results/pallas_call | solution.py:590

commit v3 on v2

--- a/solution.py
+++ b/solution.py
@@ -404,11 +404,12 @@
         grad_inner = jnp.dot(gtop[m], owt[...], preferred_element_type=F32)
         gcv[m, own, :] = (grad_inner * slope_two[m]).astype(BF16)
         halo(gcv, m, gcv_send, gcv_recv, "start")
+        if m > 0:
+            pl.when(not_low)(lambda: input_grad(m - 1, True))
+        if m == micros - 1:
+            pl.when(not_low)(lambda: input_grad(m, True))
         pl.when(is_top)(lambda: exchange_early(m))
         exchange_late(m)
-        if m > 0:
-            pl.when(not_low)(lambda: input_grad(m - 1, True))
-    pl.when(not_low)(lambda: input_grad(micros - 1, True))
 
     weight_grad(0)
 

time: 104 us -> 105 us (level); the launches traced: 103 us -> 103 us
  no operation moved by 1% of the time
where the time goes in v3:
time: 105 us; the launch traced here: 103 us
  Pallas kernels  103 us (98%)
    pallas_call x1, Pallas kernels, on_device(): pl.pallas_call(functools.partial(kernel, sizes), name='tower_backward', o...  101 us

profile of v3, /device:TPU:1, one launch (start us, length us, event | category | flops | bytes accessed | tf_op | source)
XLA Modules:
  0.0 103.2 jit_solution(15800723105605341173)
XLA Ops:
  0.6 100.5 %tower_backward.1 = (bf16[3,128,768]{2,1,0:T(8,128)(2,1)}, bf16[4,48,384]{2,1,0:T(8,128)(2,1)}) custom-call(bf16[3,128,768]{2,1,0:T(8,128)(2,1)} %bitcast.12, bf16[3,128,768]{2,1,0:T(8,128)(2,1)} %bitcast.13, bf16[3,768,384]{2,1,0:T(8,128)(2,1)} %bitcast.11, bf16[384,768]{1,0:T(8,128)(2,1)} %bitcast.14, f32[1,768]{1,0:T(1,128)} %ns_in.1, f32[1,768]{1,0:T(1,128)} %nb_in.1, ...), custom_call_target="tpu_custom_call" | custom-call | tf_op jit(solution)/shard_map/tower_backward/pallas_call | solution.py:527
  101.2 2.0 %write_results.1 = (bf16[3,128,768]{2,1,0:T(8,128)(2,1)}, f32[3,48,384]{2,1,0:T(8,128)}, f32[48,384]{1,0:T(8,128)}) custom-call(bf16[3,128,768]{2,1,0:T(8,128)(2,1)} %get-tuple-element.8.gin_in, bf16[4,48,384]{2,1,0:T(8,128)(2,1)} %get-tuple-element.9.total_in), custom_call_target="tpu_custom_call" | custom-call | tf_op jit(solution)/shard_map/write_results/pallas_call | solution.py:591

commit v4 on v2

--- a/solution.py
+++ b/solution.py
@@ -36,8 +36,9 @@
     nb_in,
     is_in,
     ib_in,
+    gin_out,
+    total_ref,
     gin_ref,
-    total_ref,
     x_ref,
     gtop,
     cw_ref,
@@ -432,6 +433,12 @@
 
     pl.when(is_low)(lambda: input_grad(micros - 1, False))
 
+    def store_gin(m):
+        return pltpu.make_async_copy(gin_ref.at[m], gin_out.at[m], load_sem.at[10 + m])
+
+    for m in range(micros):
+        store_gin(m).start()
+
     total = row[y].astype(F32)
     for t in reversed(far_first):
         y_copy(t).wait_recv()
@@ -484,6 +491,8 @@
 
     for t in far_first:
         y_copy(t).wait_send()
+    for m in range(micros):
+        store_gin(m).wait()
 
     @pl.when(jnp.logical_not(keeps))
     def _():
@@ -495,10 +504,15 @@
             spread(t).wait_send()
 
 
-def finish(factor, gin_in, total_in, gin_ref, gconv_ref, gout_ref):
-    gin_ref[...] = gin_in[...]
+def finish(factor, gin_in, total_in, gin_out, gconv_ref, gout_ref, held, sem):
+    fetch = pltpu.make_async_copy(gin_in, held, sem.at[0])
+    store = pltpu.make_async_copy(held, gin_out, sem.at[1])
+    fetch.start()
     gconv_ref[...] = total_in[:3].astype(F32) * factor
     gout_ref[...] = total_in[3].astype(F32) * factor
+    fetch.wait()
+    store.start()
+    store.wait()
 
 
 def on_device(
@@ -531,8 +545,9 @@
             jax.ShapeDtypeStruct((4, block, width), BF16),
         ),
         in_specs=[anywhere] * 8,
-        out_specs=(vmem, vmem),
+        out_specs=(anywhere, vmem),
         scratch_shapes=[
+            pltpu.VMEM((micros, rows, channels), BF16),
             pltpu.VMEM((micros, rows, channels), BF16),
             pltpu.VMEM((micros, rows, channels), BF16),
             pltpu.VMEM((3, channels, width), BF16),
@@ -556,7 +571,7 @@
             pltpu.VMEM((ny, block, width), BF16),
             pltpu.VMEM((block, width), BF16),
             pltpu.VMEM((block, width), BF16),
-            dma((10,)),
+            dma((13,)),
             dma((micros, 2)),
             dma((micros, 2)),
             dma((micros, 2)),
@@ -595,8 +610,9 @@
             jax.ShapeDtypeStruct((3, block, width), F32),
             jax.ShapeDtypeStruct((block, width), F32),
         ),
-        in_specs=[vmem] * 2,
-        out_specs=(vmem,) * 3,
+        in_specs=[anywhere, vmem],
+        out_specs=(anywhere, vmem, vmem),
+        scratch_shapes=[pltpu.VMEM((micros, rows, channels), BF16), dma((2,))],
     )(grad_in, total)
     return (
         grad_in.reshape(section_inputs.shape),

time: 104 us -> 106 us (1.019)
    pallas_call x1, Pallas kernels: 2.01 us -> 3.51 us  [on_device(): pl.pallas_call(functools.partial(finish, 1.0 / float(micros * group)), na...]
where the time goes in v4:
time: 106 us; the launch traced here: 105 us
  Pallas kernels  104 us (98%)
    pallas_call x1, Pallas kernels, on_device(): pl.pallas_call(functools.partial(kernel, sizes), name='tower_backward', o...  101 us
    pallas_call x1, Pallas kernels, on_device(): pl.pallas_call(functools.partial(finish, 1.0 / float(micros * group)), na...  3.51 us

profile of v4, /device:TPU:1, one launch (start us, length us, event | category | flops | bytes accessed | tf_op | source)
XLA Modules:
  0.0 104.8 jit_solution(2176346725900489910)
XLA Ops:
  0.6 100.6 %tower_backward.1 = (bf16[3,128,768]{2,1,0:T(8,128)(2,1)}, bf16[4,48,384]{2,1,0:T(8,128)(2,1)}) custom-call(bf16[3,128,768]{2,1,0:T(8,128)(2,1)} %bitcast.12, bf16[3,128,768]{2,1,0:T(8,128)(2,1)} %bitcast.13, bf16[3,768,384]{2,1,0:T(8,128)(2,1)} %bitcast.11, bf16[384,768]{1,0:T(8,128)(2,1)} %bitcast.14, f32[1,768]{1,0:T(1,128)} %ns_in.1, f32[1,768]{1,0:T(1,128)} %nb_in.1, ...), custom_call_target="tpu_custom_call" | custom-call | tf_op jit(solution)/shard_map/tower_backward/pallas_call | solution.py:540
  101.2 3.5 %write_results.1 = (bf16[3,128,768]{2,1,0:T(8,128)(2,1)}, f32[3,48,384]{2,1,0:T(8,128)}, f32[48,384]{1,0:T(8,128)}) custom-call(bf16[3,128,768]{2,1,0:T(8,128)(2,1)} %get-tuple-element.8.gin_in, bf16[4,48,384]{2,1,0:T(8,128)(2,1)} %get-tuple-element.9.total_in), custom_call_target="tpu_custom_call" | custom-call | tf_op jit(solution)/shard_map/write_results/pallas_call | solution.py:605

commit v5 on v2

--- a/solution.py
+++ b/solution.py
@@ -260,7 +260,7 @@
 
         lax.fori_loop(0, rows // tile, activate_inner, 0)
 
-    pieces = 3
+    pieces = 2
     piece = channels // pieces
 
     def handed(m, n):

time: 104 us -> 105 us (level)
  no operation moved by 1% of the time
where the time goes in v5:
time: 105 us; the launch traced here: 104 us
  Pallas kernels  103 us (98%)
    pallas_call x1, Pallas kernels, on_device(): pl.pallas_call(functools.partial(kernel, sizes), name='tower_backward', o...  101 us

profile of v5, /device:TPU:1, one launch (start us, length us, event | category | flops | bytes accessed | tf_op | source)
XLA Modules:
  0.0 103.8 jit_solution(9954973234778094374)
XLA Ops:
  0.6 101.2 %tower_backward.1 = (bf16[3,128,768]{2,1,0:T(8,128)(2,1)}, bf16[4,48,384]{2,1,0:T(8,128)(2,1)}) custom-call(bf16[3,128,768]{2,1,0:T(8,128)(2,1)} %bitcast.12, bf16[3,128,768]{2,1,0:T(8,128)(2,1)} %bitcast.13, bf16[3,768,384]{2,1,0:T(8,128)(2,1)} %bitcast.11, bf16[384,768]{1,0:T(8,128)(2,1)} %bitcast.14, f32[1,768]{1,0:T(1,128)} %ns_in.1, f32[1,768]{1,0:T(1,128)} %nb_in.1, ...), custom_call_target="tpu_custom_call" | custom-call | tf_op jit(solution)/shard_map/tower_backward/pallas_call | solution.py:526
  101.8 2.0 %write_results.1 = (bf16[3,128,768]{2,1,0:T(8,128)(2,1)}, f32[3,48,384]{2,1,0:T(8,128)}, f32[48,384]{1,0:T(8,128)}) custom-call(bf16[3,128,768]{2,1,0:T(8,128)(2,1)} %get-tuple-element.8.gin_in, bf16[4,48,384]{2,1,0:T(8,128)(2,1)} %get-tuple-element.9.total_in), custom_call_target="tpu_custom_call" | custom-call | tf_op jit(solution)/shard_map/write_results/pallas_call | solution.py:590

commit v6 on v2

--- a/solution.py
+++ b/solution.py
@@ -210,7 +210,7 @@
         def _():
             buffer[:, MARGIN + rows :] = zero
 
-    tile = 16
+    tile = 32
     for copy in loads_small():
         copy.wait()
 
@@ -371,6 +371,14 @@
             ]
             for copy in arrival:
                 copy.wait_recv()
+            if m == micros - 1:
+                acc[...] += lax.dot_general(
+                    lhs[m, source], rhs[m, source], TN, preferred_element_type=F32
+                )
+        if m == micros - 1:
+            last = lax.dot_general(lhs[m, dp], rhs[m, dp], TN, preferred_element_type=F32)
+            row[...] = (acc[...] + last).reshape(ny, block, width).astype(BF16)
+            return
         term = lax.dot_general(
             lhs[m].reshape(group * rows, half_c),
             rhs[m].reshape(group * rows, width),

time: 104 us -> 105 us (level)
  no operation moved by 1% of the time
where the time goes in v6:
time: 105 us; the launch traced here: 104 us
  Pallas kernels  103 us (98%)
    pallas_call x1, Pallas kernels, on_device(): pl.pallas_call(functools.partial(kernel, sizes), name='tower_backward', o...  101 us

profile of v6, /device:TPU:1, one launch (start us, length us, event | category | flops | bytes accessed | tf_op | source)
XLA Modules:
  0.0 103.8 jit_solution(15318420247634287072)
XLA Ops:
  0.6 101.2 %tower_backward.1 = (bf16[3,128,768]{2,1,0:T(8,128)(2,1)}, bf16[4,48,384]{2,1,0:T(8,128)(2,1)}) custom-call(bf16[3,128,768]{2,1,0:T(8,128)(2,1)} %bitcast.12, bf16[3,128,768]{2,1,0:T(8,128)(2,1)} %bitcast.13, bf16[3,768,384]{2,1,0:T(8,128)(2,1)} %bitcast.11, bf16[384,768]{1,0:T(8,128)(2,1)} %bitcast.14, f32[1,768]{1,0:T(1,128)} %ns_in.1, f32[1,768]{1,0:T(1,128)} %nb_in.1, ...), custom_call_target="tpu_custom_call" | custom-call | tf_op jit(solution)/shard_map/tower_backward/pallas_call | solution.py:534
  101.8 2.0 %write_results.1 = (bf16[3,128,768]{2,1,0:T(8,128)(2,1)}, f32[3,48,384]{2,1,0:T(8,128)}, f32[48,384]{1,0:T(8,128)}) custom-call(bf16[3,128,768]{2,1,0:T(8,128)(2,1)} %get-tuple-element.8.gin_in, bf16[4,48,384]{2,1,0:T(8,128)(2,1)} %get-tuple-element.9.total_in), custom_call_target="tpu_custom_call" | custom-call | tf_op jit(solution)/shard_map/write_results/pallas_call | solution.py:598
